TPU v7x, 256 devices: a whole 4x4x8 slice. The times are simulated.
256 devices in a mesh: px: 16 (over y, x), py: 16 (over z, core).
Axes of the slice: x: 4, y: 4, z: 8, core: 2. Of those that a mesh axis runs over, the one named last changes fastest.
Arguments:
- start_field: float32 [128, 256, 512], P('px', 'py'), may hold values from -1.7 to 1.7
- known: float32 [8, 128, 256, 512], P(None, 'px', 'py'), may hold values from -1 to 1
Outputs:
- solution_field: float32 [128, 256, 512], P('px', 'py')
- residual: float32 [128, 256, 512], P('px', 'py')
All inputs are finite; a program needn't handle non-finite values.
Results may differ from a plain program's by a relative error of at most 0.01.
Values sent between devices are 32-bit elements; how exact they have to be, the bound alone decides.
No kernel may reach another device: no remote copies, remote signals or barrier semaphores. Data moves between devices by JAX's collectives and lax.ppermute only.
A program may use at most 64 MiB of HBM per device.

v0:
```python
import jax
import jax.numpy as jnp
from jax import lax
from jax.sharding import PartitionSpec as P

NEWTON = 2
ITERS = 3
DIFFUSION = 0.5
SHIFT = 4.0
EPS = 1e-06


def extended(cells, sides, width):
    for axis, dim in sides:
        count = lax.axis_size(axis)
        ends = count - 1
        head = lax.slice_in_dim(cells, 0, width, axis=dim)
        tail = lax.slice_in_dim(cells, cells.shape[dim] - width, cells.shape[dim], axis=dim)
        cells = jnp.concatenate(
            [
                lax.ppermute(tail, axis, [(i, (i + 1) % count) for i in range(ends)]),
                cells,
                lax.ppermute(head, axis, [((i + 1) % count, i) for i in range(ends)]),
            ],
            axis=dim,
        )
    return cells


def laplace(field):
    padded = extended(field, (("px", 0), ("py", 1)), 1)
    zero = jnp.zeros_like(field[:, :, :1])
    upper = jnp.concatenate([field[:, :, 1:], zero], axis=2)
    lower = jnp.concatenate([zero, field[:, :, :-1]], axis=2)
    beside = padded[2:, 1:-1, :] + padded[:-2, 1:-1, :]
    beside = beside + padded[1:-1, 2:, :] + padded[1:-1, :-2, :]
    return beside + upper + lower - 6.0 * field


def allen_cahn(field, lap):
    return DIFFUSION * lap + field - field * field * field


def solve_small(hess, beta):
    normal = jnp.sum(hess[:, :, None] * hess[:, None, :], axis=0)
    target = beta * hess[0]
    lower = jnp.linalg.cholesky(normal)
    count = normal.shape[0]
    forward = []
    for i in range(count):
        acc = target[i]
        for j in range(i):
            acc = acc - lower[i, j] * forward[j]
        forward.append(acc / lower[i, i])
    back = [None] * count
    for i in reversed(range(count)):
        acc = forward[i]
        for j in range(i + 1, count):
            acc = acc - lower[j, i] * back[j]
        back[i] = acc / lower[i, i]
    return jnp.stack(back)


def local(start_field, known):
    cells = float(
        start_field.shape[0]
        * lax.axis_size("px")
        * start_field.shape[1]
        * lax.axis_size("py")
        * start_field.shape[2]
    )
    field = start_field
    lap_field = laplace(field)
    for step in range(NEWTON):
        force = allen_cahn(field, lap_field)
        diffs = field[None] - known
        dist_local = jnp.sum(diffs * diffs, axis=(1, 2, 3))
        first_sum, force_sq = lax.psum((dist_local, jnp.sum(force * force)), ("px", "py"))
        beta = jnp.sqrt(force_sq + EPS)
        basis = [-force / beta]
        lap_basis = []
        jac_diag = 1.0 - 3.0 * field * field
        hess = jnp.zeros((ITERS + 1, ITERS), jnp.float32)
        for k in range(ITERS):
            lap_vec = laplace(basis[k])
            lap_basis.append(lap_vec)
            image = DIFFUSION * lap_vec + jac_diag * basis[k]
            heights_local = jnp.stack([jnp.sum(vec * image) for vec in basis])
            summed = lax.psum(heights_local, ("px", "py"))
            rest = image
            for j in range(k + 1):
                rest = rest - summed[j] * basis[j]
            height = jnp.sqrt(lax.psum(jnp.sum(rest * rest), ("px", "py")) + EPS)
            hess = hess.at[: k + 1, k].set(summed).at[k + 1, k].set(height)
            if k < ITERS - 1:
                basis.append(rest / height)
        coeffs = solve_small(hess, beta)
        delta = coeffs[0] * basis[0]
        for j in range(1, ITERS):
            delta = delta + coeffs[j] * basis[j]
        inner = lax.psum(jnp.sum(diffs * delta[None], axis=(1, 2, 3)), ("px", "py"))
        mean_dist = first_sum / cells + EPS
        weight = 1.0 / mean_dist + SHIFT
        total = jnp.sum(2.0 * inner / (cells * mean_dist * mean_dist * weight))
        scale = 1.0 / (1.0 + jnp.abs(total))
        field = field + scale * delta
        lap_field = laplace(field)
    return (field, allen_cahn(field, lap_field))


def solution(mesh):
    placed = (P("px", "py", None), P(None, "px", "py", None))
    return jax.shard_map(
        local,
        mesh=mesh,
        in_specs=placed,
        out_specs=(P("px", "py", None), P("px", "py", None)),
        check_vma=False,
    )
```

profile of v0, /device:TPU:38, one launch (start us, length us, event | category | flops | bytes accessed | tf_op | source)
XLA Modules:
  0.0 1435.6 jit_solution(6165251050151356504)
XLA Ops:
  1.5 2.7 collective-permute-start
  4.2 5.2 collective-permute-start.1
  19.9 80.0 %psum.126 = f32[]{:T(128)} all-reduce(f32[]{:T(128)} %get-tuple-element.179), channel_id=1, replica_groups=mesh['px'=16,'py'=16] {'px','py'}, use_global_device_ids=true, to_apply=%region_1.0 | all-reduce | flops 1 | bytes 8 | tf_op jit(solution)/shard_map/psum | solution.py:78
  100.6 3.4 collective-permute-start.5
  104.0 2.5 collective-permute-start.4
  107.2 4.7 collective-permute-done.4
  116.5 2.5 collective-permute-done.7
  119.8 73.3 %psum.127 = f32[1]{0:T(128)} all-reduce(f32[1]{0:T(128)} %bitcast), channel_id=1, replica_groups=mesh['px'=16,'py'=16] {'px','py'}, use_global_device_ids=true, to_apply=%region_3.0 | all-reduce | flops 1 | bytes 8 | tf_op jit(solution)/shard_map/psum | solution.py:89
  194.5 74.3 %psum.128 = f32[]{:T(128)} all-reduce(f32[]{:T(128)} %multiply_reduce_fusion.21), channel_id=1, replica_groups=mesh['px'=16,'py'=16] {'px','py'}, use_global_device_ids=true, to_apply=%region_5.0 | all-reduce | flops 1 | bytes 8 | tf_op jit(solution)/shard_map/psum | solution.py:93
  270.2 3.4 collective-permute-start.9
  273.6 2.5 collective-permute-start.8
  277.3 4.1 collective-permute-done.8
  291.0 73.4 %psum.129 = f32[2]{0:T(128)S(1)} all-reduce(f32[2]{0:T(128)S(1)} %pad_maximum_fusion.92), channel_id=1, replica_groups=mesh['px'=16,'py'=16] {'px','py'}, use_global_device_ids=true, to_apply=%region_9.0 | all-reduce | flops 2 | bytes 16 | tf_op jit(solution)/shard_map/psum | solution.py:89
  367.1 74.1 %psum.130 = f32[]{:T(128)} all-reduce(f32[]{:T(128)} %get-tuple-element.174), channel_id=1, replica_groups=mesh['px'=16,'py'=16] {'px','py'}, use_global_device_ids=true, to_apply=%region_11.0 | all-reduce | flops 1 | bytes 8 | tf_op jit(solution)/shard_map/psum | solution.py:93
  441.9 3.4 collective-permute-start.13
  448.6 4.6 collective-permute-done.12
  461.1 2.8 multiply_reduce_fusion.17
  466.0 75.2 %psum.131 = f32[3]{0:T(128)S(1)} all-reduce(f32[3]{0:T(128)S(1)} %pad_maximum_fusion.93), channel_id=1, replica_groups=mesh['px'=16,'py'=16] {'px','py'}, use_global_device_ids=true, to_apply=%region_16.0 | all-reduce | flops 3 | bytes 24 | tf_op jit(solution)/shard_map/psum | solution.py:89
  543.7 3.6 multiply_reduce_fusion.14
  548.8 74.0 %psum.132 = f32[]{:T(128)} all-reduce(f32[]{:T(128)} %multiply_reduce_fusion.14), channel_id=1, replica_groups=mesh['px'=16,'py'=16] {'px','py'}, use_global_device_ids=true, to_apply=%region_18.0 | all-reduce | flops 1 | bytes 8 | tf_op jit(solution)/shard_map/psum | solution.py:93
  636.7 73.7 %all-reduce.21 = (f32[8]{0:T(128)S(1)}, f32[8]{0:T(128)S(1)}) all-reduce(f32[8]{0:T(128)S(1)} %get-tuple-element.150, f32[8]{0:T(128)S(1)} %get-tuple-element.149), channel_id=1, replica_groups=mesh['px'=16,'py'=16] {'px','py'}, use_global_device_ids=true, to_apply=%region_25.27 | all-reduce | flops 16 | bytes 128 | tf_op jit(solution)/shard_map/psum | solution.py:78
  711.9 3.3 collective-permute-start.17
  715.2 2.5 collective-permute-start.16
  717.7 5.4 collective-permute-done.16
  727.6 2.5 collective-permute-done.19
  731.0 73.4 %psum.135 = f32[]{:T(128)} all-reduce(f32[]{:T(128)} %get-tuple-element.171), channel_id=1, replica_groups=mesh['px'=16,'py'=16] {'px','py'}, use_global_device_ids=true, to_apply=%region_28.0 | all-reduce | flops 1 | bytes 8 | tf_op jit(solution)/shard_map/psum | solution.py:78
  805.1 3.4 collective-permute-start.21
  808.5 2.5 collective-permute-start.20
  811.0 5.4 collective-permute-done.20
  820.9 2.5 collective-permute-done.23
  824.3 73.4 %psum.136 = f32[1]{0:T(128)} all-reduce(f32[1]{0:T(128)} %bitcast.32), channel_id=1, replica_groups=mesh['px'=16,'py'=16] {'px','py'}, use_global_device_ids=true, to_apply=%region_30.0 | all-reduce | flops 1 | bytes 8 | tf_op jit(solution)/shard_map/psum | solution.py:89
  899.0 74.1 %psum.137 = f32[]{:T(128)} all-reduce(f32[]{:T(128)} %multiply_reduce_fusion.11), channel_id=1, replica_groups=mesh['px'=16,'py'=16] {'px','py'}, use_global_device_ids=true, to_apply=%region_32.0 | all-reduce | flops 1 | bytes 8 | tf_op jit(solution)/shard_map/psum | solution.py:93
  974.5 3.4 collective-permute-start.25
  977.9 2.5 collective-permute-start.24
  980.4 5.4 collective-permute-done.24
  995.3 73.4 %psum.138 = f32[2]{0:T(128)S(1)} all-reduce(f32[2]{0:T(128)S(1)} %pad_maximum_fusion.94), channel_id=1, replica_groups=mesh['px'=16,'py'=16] {'px','py'}, use_global_device_ids=true, to_apply=%region_35.0 | all-reduce | flops 2 | bytes 16 | tf_op jit(solution)/shard_map/psum | solution.py:89
  1071.4 74.0 %psum.139 = f32[]{:T(128)} all-reduce(f32[]{:T(128)} %get-tuple-element.166), channel_id=1, replica_groups=mesh['px'=16,'py'=16] {'px','py'}, use_global_device_ids=true, to_apply=%region_37.0 | all-reduce | flops 1 | bytes 8 | tf_op jit(solution)/shard_map/psum | solution.py:93
  1146.1 3.4 collective-permute-start.29
  1152.9 4.6 collective-permute-done.28
  1166.0 2.7 multiply_reduce_fusion.7
  1170.8 75.2 %psum.140 = f32[3]{0:T(128)S(1)} all-reduce(f32[3]{0:T(128)S(1)} %pad_maximum_fusion.95), channel_id=1, replica_groups=mesh['px'=16,'py'=16] {'px','py'}, use_global_device_ids=true, to_apply=%region_41.0 | all-reduce | flops 3 | bytes 24 | tf_op jit(solution)/shard_map/psum | solution.py:89
  1248.5 3.6 multiply_reduce_fusion.4
  1253.5 74.1 %psum.141 = f32[]{:T(128)} all-reduce(f32[]{:T(128)} %multiply_reduce_fusion.4), channel_id=1, replica_groups=mesh['px'=16,'py'=16] {'px','py'}, use_global_device_ids=true, to_apply=%region_43.0 | all-reduce | flops 1 | bytes 8 | tf_op jit(solution)/shard_map/psum | solution.py:93
  1341.6 73.5 %all-reduce.20 = (f32[8]{0:T(128)S(1)}, f32[8]{0:T(128)S(1)}) all-reduce(f32[8]{0:T(128)S(1)} %get-tuple-element.148, f32[8]{0:T(128)S(1)} %get-tuple-element.147), channel_id=1, replica_groups=mesh['px'=16,'py'=16] {'px','py'}, use_global_device_ids=true, to_apply=%region_48.0 | all-reduce | flops 16 | bytes 128 | tf_op jit(solution)/shard_map/psum | solution.py:78
  1416.4 3.3 collective-permute-start.33
  1419.8 2.5 collective-permute-start.32
  1422.3 5.4 collective-permute-done.32
  1432.2 2.5 collective-permute-done.35
  (157 shorter events, 107.0 us)
Async XLA Ops:
  0.6 18.4 %copy-start = (f32[8,16,512]{2,1,0:T(8,128)S(1)}, f32[8,16,512]{2,1,0:T(8,128)}, u32[]{:S(2)}) copy-start(f32[8,16,512]{2,1,0:T(8,128)} %param.27) | copy-start | bytes 786436
  1.5 10.5 collective-permute-start
  4.2 6.8 collective-permute-start.1
  12.0 5.6 collective-permute-start.2
  14.0 5.1 collective-permute-start.3
  100.6 6.5 collective-permute-start.5
  104.0 7.9 collective-permute-start.4
  112.0 4.5 collective-permute-start.6
  113.9 5.1 collective-permute-start.7
  270.2 7.1 collective-permute-start.9
  273.6 7.9 collective-permute-start.8
  281.5 5.1 collective-permute-start.10
  283.4 5.1 collective-permute-start.11
  441.9 6.7 collective-permute-start.13
  445.3 7.9 collective-permute-start.12
  453.2 7.9 collective-permute-start.14
  455.1 6.0 collective-permute-start.15
  461.1 175.0 %copy-start.1 = (f32[8,8,16,512]{3,2,1,0:T(8,128)S(1)}, f32[8,8,16,512]{3,2,1,0:T(8,128)}, u32[]{:S(2)}) copy-start(f32[8,8,16,512]{3,2,1,0:T(8,128)} %param.28) | copy-start | bytes 6291460
  711.9 5.9 collective-permute-start.17
  715.2 7.9 collective-permute-start.16
  723.1 4.5 collective-permute-start.18
  725.0 5.1 collective-permute-start.19
  805.1 5.9 collective-permute-start.21
  808.5 7.9 collective-permute-start.20
  816.4 4.5 collective-permute-start.22
  818.3 5.1 collective-permute-start.23
  974.5 5.9 collective-permute-start.25
  977.9 7.9 collective-permute-start.24
  985.8 5.1 collective-permute-start.26
  987.8 5.1 collective-permute-start.27
  1146.1 6.7 collective-permute-start.29
  1149.5 7.9 collective-permute-start.28
  1158.1 7.9 collective-permute-start.30
  1160.0 6.0 collective-permute-start.31
  1416.4 19.2 %copy-start.2 = (f32[8,16,512]{2,1,0:T(8,128)}, f32[8,16,512]{2,1,0:T(8,128)S(1)}, u32[]{:S(2)}) copy-start(f32[8,16,512]{2,1,0:T(8,128)S(1)} %multiply_add_fusion) | copy-start | bytes 786436
  1416.4 5.9 collective-permute-start.33
  1419.8 7.9 collective-permute-start.32
  1427.7 4.5 collective-permute-start.34
  1429.6 5.1 collective-permute-start.35
where the time goes:
time: 1440 us
  blocking collectives  1190 us (83%)
  starting transfers between devices  93.6 us (6%)
  waiting for transfers between devices  55.3 us (4%)
  other arithmetic  50.1 us (3%)
  between operations  27.2 us (2%)
  local copies, waits for them, and re-layouts  20.1 us (1%)
    psum x6, blocking collectives, local(): height = jnp.sqrt(lax.psum(jnp.sum(rest * rest), ('px', 'py')) + EPS)  445 us
    psum x6, blocking collectives, local(): summed = lax.psum(heights_local, ('px', 'py'))  444 us
    psum x4, blocking collectives, local(): lax.psum((dist_local, jnp.sum(force * force)), ('px', 'py'))  301 us
    ppermute x18, starting transfers between devices, extended(): lax.ppermute(tail, axis, [(i, (i + 1) % count) for i in range(ends)])  53.6 us
    ppermute x18, starting transfers between devices, extended(): lax.ppermute(head, axis, [((i + 1) % count, i) for i in range(ends)])  40 us
    ppermute x18, waiting for transfers between devices, extended(): lax.ppermute(head, axis, [((i + 1) % count, i) for i in range(ends)])  39.6 us
  transfers between devices with their start and end apart: 36, of which 16 were waited for; matrix products, arithmetic and copies ran while one was open for 1% of the time, Pallas kernels for 0%

commit v1 on v0

--- a/solution.py
+++ b/solution.py
@@ -86,7 +86,9 @@
             lap_basis.append(lap_vec)
             image = DIFFUSION * lap_vec + jac_diag * basis[k]
             heights_local = jnp.stack([jnp.sum(vec * image) for vec in basis])
-            summed = lax.psum(heights_local, ("px", "py"))
+            summed = heights_local
+            for mesh_axis in ("py", "px"):
+                summed = lax.psum(summed, mesh_axis)
             rest = image
             for j in range(k + 1):
                 rest = rest - summed[j] * basis[j]

time: 1440 us -> 1330 us (0.924)
  blocking collectives: 1190 us -> 1080 us
    psum x6 -> x12, blocking collectives: 444 us -> 312 us  [local(): summed = lax.psum(summed, mesh_axis)]
    psum x6, blocking collectives: 445 us -> 475 us  [local(): height = jnp.sqrt(lax.psum(jnp.sum(rest * rest), ('px', 'py')) + EPS)]
  transfers between devices with their start and end apart: 36 -> 36, of which waited for: 16 -> 18; matrix products, arithmetic and copies ran while one was open for 1% -> 1% of each run, Pallas kernels for 0% -> 0%
where the time goes in v1:
time: 1330 us
  blocking collectives  1080 us (81%)
  starting transfers between devices  91.7 us (7%)
  waiting for transfers between devices  64.5 us (5%)
  other arithmetic  42.9 us (3%)
  between operations  27.6 us (2%)
  local copies, waits for them, and re-layouts  18.4 us (1%)
    psum x6, blocking collectives, local(): height = jnp.sqrt(lax.psum(jnp.sum(rest * rest), ('px', 'py')) + EPS)  475 us
    psum x12, blocking collectives, local(): summed = lax.psum(summed, mesh_axis)  312 us
    psum x4, blocking collectives, local(): lax.psum((dist_local, jnp.sum(force * force)), ('px', 'py'))  297 us
    ppermute x18, starting transfers between devices, extended(): lax.ppermute(tail, axis, [(i, (i + 1) % count) for i in range(ends)])  51.8 us
    ppermute x18, waiting for transfers between devices, extended(): lax.ppermute(head, axis, [((i + 1) % count, i) for i in range(ends)])  45.5 us
    ppermute x18, starting transfers between devices, extended(): lax.ppermute(head, axis, [((i + 1) % count, i) for i in range(ends)])  39.9 us
  transfers between devices with their start and end apart: 36, of which 18 were waited for; matrix products, arithmetic and copies ran while one was open for 1% of the time, Pallas kernels for 0%

profile of v1, /device:TPU:38, one launch (start us, length us, event | category | flops | bytes accessed | tf_op | source)
XLA Modules:
  0.0 1329.2 jit_solution(2875090072559103735)
XLA Ops:
  1.5 3.4 collective-permute-start.1
  8.3 4.5 collective-permute-done
  20.7 76.6 %psum.168 = f32[]{:T(128)} all-reduce(f32[]{:T(128)} %get-tuple-element.179), channel_id=1, replica_groups=mesh['px'=16,'py'=16] {'px','py'}, use_global_device_ids=true, to_apply=%region_1.0 | all-reduce | flops 1 | bytes 8 | tf_op jit(solution)/shard_map/psum | solution.py:78
  98.1 3.4 collective-permute-start.5
  104.6 4.7 collective-permute-done.4
  113.9 2.5 collective-permute-done.7
  117.2 21.3 %psum.169 = f32[1]{0:T(128)} all-reduce(f32[1]{0:T(128)} %bitcast), channel_id=1, replica_groups=mesh['px'=16,'py'=16] {'py'}, use_global_device_ids=true, to_apply=%region_3.0 | all-reduce | flops 1 | bytes 8 | tf_op jit(solution)/shard_map/psum | solution.py:91
  139.2 31.0 %psum.170 = f32[1]{0:T(128)} all-reduce(f32[1]{0:T(128)} %psum.169), channel_id=1, replica_groups=mesh['px'=16,'py'=16] {'px'}, use_global_device_ids=true, to_apply=%region_4.0 | all-reduce | flops 1 | bytes 8 | tf_op jit(solution)/shard_map/psum | solution.py:91
  171.5 79.2 %psum.171 = f32[]{:T(128)} all-reduce(f32[]{:T(128)} %multiply_reduce_fusion.21), channel_id=1, replica_groups=mesh['px'=16,'py'=16] {'px','py'}, use_global_device_ids=true, to_apply=%region_6.0 | all-reduce | flops 1 | bytes 8 | tf_op jit(solution)/shard_map/psum | solution.py:95
  252.1 3.4 collective-permute-start.9
  259.3 4.1 collective-permute-done.8
  267.9 2.5 collective-permute-done.11
  273.4 21.4 %psum.172 = f32[2]{0:T(128)S(1)} all-reduce(f32[2]{0:T(128)S(1)} %pad_maximum_fusion.92), channel_id=1, replica_groups=mesh['px'=16,'py'=16] {'py'}, use_global_device_ids=true, to_apply=%region_10.0 | all-reduce | flops 2 | bytes 16 | tf_op jit(solution)/shard_map/psum | solution.py:91
  294.8 30.4 %psum.173 = f32[2]{0:T(128)S(1)} all-reduce(f32[2]{0:T(128)S(1)} %psum.172), channel_id=1, replica_groups=mesh['px'=16,'py'=16] {'px'}, use_global_device_ids=true, to_apply=%region_11.0 | all-reduce | flops 2 | bytes 16 | tf_op jit(solution)/shard_map/psum | solution.py:91
  327.7 79.2 %psum.174 = f32[]{:T(128)} all-reduce(f32[]{:T(128)} %get-tuple-element.174), channel_id=1, replica_groups=mesh['px'=16,'py'=16] {'px','py'}, use_global_device_ids=true, to_apply=%region_13.0 | all-reduce | flops 1 | bytes 8 | tf_op jit(solution)/shard_map/psum | solution.py:95
  407.7 3.4 collective-permute-start.13
  413.7 5.3 collective-permute-done.12
  430.3 21.5 %psum.175 = f32[3]{0:T(128)S(1)} all-reduce(f32[3]{0:T(128)S(1)} %pad_maximum_fusion.93), channel_id=1, replica_groups=mesh['px'=16,'py'=16] {'py'}, use_global_device_ids=true, to_apply=%region_18.0 | all-reduce | flops 3 | bytes 24 | tf_op jit(solution)/shard_map/psum | solution.py:91
  452.0 30.4 %psum.176 = f32[3]{0:T(128)S(1)} all-reduce(f32[3]{0:T(128)S(1)} %psum.175), channel_id=1, replica_groups=mesh['px'=16,'py'=16] {'px'}, use_global_device_ids=true, to_apply=%region_19.0 | all-reduce | flops 3 | bytes 24 | tf_op jit(solution)/shard_map/psum | solution.py:91
  485.0 2.6 multiply_reduce_fusion.14
  489.0 78.9 %psum.177 = f32[]{:T(128)} all-reduce(f32[]{:T(128)} %multiply_reduce_fusion.14), channel_id=1, replica_groups=mesh['px'=16,'py'=16] {'px','py'}, use_global_device_ids=true, to_apply=%region_21.0 | all-reduce | flops 1 | bytes 8 | tf_op jit(solution)/shard_map/psum | solution.py:95
  582.1 73.4 %all-reduce.21 = (f32[8]{0:T(128)S(1)}, f32[8]{0:T(128)S(1)}) all-reduce(f32[8]{0:T(128)S(1)} %get-tuple-element.150, f32[8]{0:T(128)S(1)} %get-tuple-element.149), channel_id=1, replica_groups=mesh['px'=16,'py'=16] {'px','py'}, use_global_device_ids=true, to_apply=%region_28.30 | all-reduce | flops 16 | bytes 128 | tf_op jit(solution)/shard_map/psum | solution.py:78
  656.8 3.3 collective-permute-start.17
  660.1 2.5 collective-permute-start.16
  662.7 5.4 collective-permute-done.16
  672.6 3.0 collective-permute-done.19
  676.4 73.7 %psum.180 = f32[]{:T(128)} all-reduce(f32[]{:T(128)} %get-tuple-element.171), channel_id=1, replica_groups=mesh['px'=16,'py'=16] {'px','py'}, use_global_device_ids=true, to_apply=%region_31.0 | all-reduce | flops 1 | bytes 8 | tf_op jit(solution)/shard_map/psum | solution.py:78
  750.8 3.4 collective-permute-start.21
  756.6 5.4 collective-permute-done.20
  766.8 2.5 collective-permute-done.23
  770.1 21.4 %psum.181 = f32[1]{0:T(128)} all-reduce(f32[1]{0:T(128)} %bitcast.32), channel_id=1, replica_groups=mesh['px'=16,'py'=16] {'py'}, use_global_device_ids=true, to_apply=%region_33.0 | all-reduce | flops 1 | bytes 8 | tf_op jit(solution)/shard_map/psum | solution.py:91
  791.5 31.2 %psum.182 = f32[1]{0:T(128)} all-reduce(f32[1]{0:T(128)} %psum.181), channel_id=1, replica_groups=mesh['px'=16,'py'=16] {'px'}, use_global_device_ids=true, to_apply=%region_34.0 | all-reduce | flops 1 | bytes 8 | tf_op jit(solution)/shard_map/psum | solution.py:91
  824.0 79.6 %psum.183 = f32[]{:T(128)} all-reduce(f32[]{:T(128)} %multiply_reduce_fusion.11), channel_id=1, replica_groups=mesh['px'=16,'py'=16] {'px','py'}, use_global_device_ids=true, to_apply=%region_36.0 | all-reduce | flops 1 | bytes 8 | tf_op jit(solution)/shard_map/psum | solution.py:95
  905.0 3.4 collective-permute-start.25
  910.9 5.4 collective-permute-done.24
  926.3 21.4 %psum.184 = f32[2]{0:T(128)S(1)} all-reduce(f32[2]{0:T(128)S(1)} %pad_maximum_fusion.94), channel_id=1, replica_groups=mesh['px'=16,'py'=16] {'py'}, use_global_device_ids=true, to_apply=%region_39.0 | all-reduce | flops 2 | bytes 16 | tf_op jit(solution)/shard_map/psum | solution.py:91
  947.8 30.4 %psum.185 = f32[2]{0:T(128)S(1)} all-reduce(f32[2]{0:T(128)S(1)} %psum.184), channel_id=1, replica_groups=mesh['px'=16,'py'=16] {'px'}, use_global_device_ids=true, to_apply=%region_40.0 | all-reduce | flops 2 | bytes 16 | tf_op jit(solution)/shard_map/psum | solution.py:91
  980.7 78.6 %psum.186 = f32[]{:T(128)} all-reduce(f32[]{:T(128)} %get-tuple-element.166), channel_id=1, replica_groups=mesh['px'=16,'py'=16] {'px','py'}, use_global_device_ids=true, to_apply=%region_42.0 | all-reduce | flops 1 | bytes 8 | tf_op jit(solution)/shard_map/psum | solution.py:95
  1060.0 3.4 collective-permute-start.29
  1066.0 5.3 collective-permute-done.28
  1082.5 21.5 %psum.187 = f32[3]{0:T(128)S(1)} all-reduce(f32[3]{0:T(128)S(1)} %pad_maximum_fusion.95), channel_id=1, replica_groups=mesh['px'=16,'py'=16] {'py'}, use_global_device_ids=true, to_apply=%region_46.0 | all-reduce | flops 3 | bytes 24 | tf_op jit(solution)/shard_map/psum | solution.py:91
  1104.2 30.4 %psum.188 = f32[3]{0:T(128)S(1)} all-reduce(f32[3]{0:T(128)S(1)} %psum.187), channel_id=1, replica_groups=mesh['px'=16,'py'=16] {'px'}, use_global_device_ids=true, to_apply=%region_47.0 | all-reduce | flops 3 | bytes 24 | tf_op jit(solution)/shard_map/psum | solution.py:91
  1137.1 2.6 multiply_reduce_fusion.4
  1141.2 79.4 %psum.189 = f32[]{:T(128)} all-reduce(f32[]{:T(128)} %multiply_reduce_fusion.4), channel_id=1, replica_groups=mesh['px'=16,'py'=16] {'px','py'}, use_global_device_ids=true, to_apply=%region_49.0 | all-reduce | flops 1 | bytes 8 | tf_op jit(solution)/shard_map/psum | solution.py:95
  1234.8 73.4 %all-reduce.20 = (f32[8]{0:T(128)S(1)}, f32[8]{0:T(128)S(1)}) all-reduce(f32[8]{0:T(128)S(1)} %get-tuple-element.148, f32[8]{0:T(128)S(1)} %get-tuple-element.147), channel_id=1, replica_groups=mesh['px'=16,'py'=16] {'px','py'}, use_global_device_ids=true, to_apply=%region_54.0 | all-reduce | flops 16 | bytes 128 | tf_op jit(solution)/shard_map/psum | solution.py:78
  1309.6 3.3 collective-permute-start.33
  1315.4 5.4 collective-permute-done.32
  1325.4 2.9 collective-permute-done.35
  (165 shorter events, 120.7 us)
Async XLA Ops:
  0.6 103.3 %copy-start.3 = (s32[2]{0:T(128)S(1)}, s32[2]{0:T(128)}, u32[]{:S(2)}) copy-start(s32[2]{0:T(128)} %constant.311.clone.1) | copy-start | bytes 28
  0.6 19.2 %copy-start = (f32[8,16,512]{2,1,0:T(8,128)S(1)}, f32[8,16,512]{2,1,0:T(8,128)}, u32[]{:S(2)}) copy-start(f32[8,16,512]{2,1,0:T(8,128)} %param.27) | copy-start | bytes 786436
  1.5 5.8 collective-permute-start.1
  4.9 7.9 collective-permute-start
  12.8 5.5 collective-permute-start.2
  14.8 5.1 collective-permute-start.3
  98.1 6.5 collective-permute-start.5
  101.4 7.9 collective-permute-start.4
  109.4 4.5 collective-permute-start.6
  111.3 5.1 collective-permute-start.7
  252.1 7.2 collective-permute-start.9
  255.5 7.9 collective-permute-start.8
  263.4 4.5 collective-permute-start.10
  265.3 5.1 collective-permute-start.11
  407.7 6.0 collective-permute-start.13
  411.0 7.9 collective-permute-start.12
  419.0 6.3 collective-permute-start.14
  420.9 5.1 collective-permute-start.15
  426.0 155.5 %copy-start.1 = (f32[8,8,16,512]{3,2,1,0:T(8,128)S(1)}, f32[8,8,16,512]{3,2,1,0:T(8,128)}, u32[]{:S(2)}) copy-start(f32[8,8,16,512]{3,2,1,0:T(8,128)} %param.28) | copy-start | bytes 6291460
  656.8 5.9 collective-permute-start.17
  660.1 7.9 collective-permute-start.16
  668.1 4.5 collective-permute-start.18
  670.1 5.5 collective-permute-start.19
  750.8 5.9 collective-permute-start.21
  754.1 7.9 collective-permute-start.20
  762.1 4.7 collective-permute-start.22
  764.2 5.1 collective-permute-start.23
  905.0 5.9 collective-permute-start.25
  908.4 7.9 collective-permute-start.24
  916.3 4.5 collective-permute-start.26
  918.3 5.1 collective-permute-start.27
  1060.0 6.0 collective-permute-start.29
  1063.4 7.9 collective-permute-start.28
  1071.3 6.3 collective-permute-start.30
  1073.2 5.1 collective-permute-start.31
  1309.5 19.6 %copy-start.2 = (f32[8,16,512]{2,1,0:T(8,128)}, f32[8,16,512]{2,1,0:T(8,128)S(1)}, u32[]{:S(2)}) copy-start(f32[8,16,512]{2,1,0:T(8,128)S(1)} %multiply_add_fusion) | copy-start | bytes 786436
  1309.6 5.9 collective-permute-start.33
  1312.9 7.9 collective-permute-start.32
  1320.9 4.5 collective-permute-start.34
  1322.8 5.5 collective-permute-start.35
